TPU v7x, 32 devices: a whole 2x2x4 slice. The times are simulated.
32 devices in a mesh: gx: 4 (over z), gy: 8 (over y, x, core).
Axes of the slice: x: 2, y: 2, z: 4, core: 2. Of those that a mesh axis runs over, the one named last changes fastest.
Arguments:
- right_side: float32 [32, 128, 128], P('gx', 'gy'), may hold values from -8 to 8
- diagonal: float32 [32, 128, 128], P('gx', 'gy'), may hold values from 0.25 to 2
- solid_mask: int32 [32, 128, 128], P('gx', 'gy'), may hold values 0 or 1
- geneo_vectors: bfloat16 [32, 32, 128, 128], P(None, 'gx', 'gy'), may hold values from -0.046875 to 0.046875
- vector_counts: int32 [4, 8], P('gx', 'gy'), may hold values from 8 to 32, as said below
- owner_slots: int32 [32], replicated, may hold values from 0 to 31, each once
- coarse_inverse: float32 [1024, 64], P('gy'), may hold values from -1 to 8, as said below
Outputs:
- solution: float32 [32, 128, 128], P('gx', 'gy')
- residual: float32 [32, 128, 128], P('gx', 'gy')
Inputs may be any that keep to these rules, and one draw needn't show every extreme that they name: `vector_counts`: every count lies between 8 and 32; both ends occur in every draw. Subdomain s belongs to coarse block owner_slots[s] // 2. `coarse_inverse`: each block is symmetric positive definite; rows and columns beyond a subdomain's count are unused.
All inputs are finite; a program needn't handle non-finite values. No bound on the sum of `solid_mask` on one device may be relied on, other than what follows from the above.
Results may differ from a plain program's by a relative error of at most 0.0003.
Values sent between devices are 32-bit elements; how exact they have to be, the bound alone decides.
No kernel may reach another device: no remote copies, remote signals or barrier semaphores. Data moves between devices by JAX's collectives and lax.ppermute only.
A program may use at most 64 MiB of HBM per device.

v0:
```python
import jax
import jax.numpy as jnp
from jax import lax
from jax.sharding import PartitionSpec as P

DEG = 3
ITERS = 2
CHEB_LO = 0.3
CHEB_HI = 2.0
HIGH = lax.Precision.HIGHEST


def with_halo(cells, sides, width):
    for axis, dim in sides:
        count = lax.axis_size(axis)
        ends = count - 1
        head = lax.slice_in_dim(cells, 0, width, axis=dim)
        tail = lax.slice_in_dim(cells, cells.shape[dim] - width, cells.shape[dim], axis=dim)
        cells = jnp.concatenate(
            [
                lax.ppermute(tail, axis, [(i, (i + 1) % count) for i in range(ends)]),
                cells,
                lax.ppermute(head, axis, [((i + 1) % count, i) for i in range(ends)]),
            ],
            axis=dim,
        )
    return cells


def operate(field, diagonal, fluid):
    masked = fluid * field
    padded = with_halo(masked, (("gx", 0), ("gy", 1)), 1)
    beside = padded[2:, 1:-1] + padded[:-2, 1:-1] + padded[1:-1, 2:] + padded[1:-1, :-2]
    vertical = jnp.pad(masked, ((0, 0), (0, 0), (1, 1)))
    beside = beside + vertical[:, :, 2:] + vertical[:, :, :-2]
    return fluid * ((6.0 + diagonal) * field - beside) + (1.0 - fluid) * field


def smoother(res, diagonal, fluid, jacobi):
    centre = (CHEB_HI + CHEB_LO) / 2.0
    half_width = (CHEB_HI - CHEB_LO) / 2.0
    sigma_val = centre / half_width
    rho_old = 1.0 / sigma_val
    update = jacobi * res / centre
    smooth = update
    remainder = res
    for repeat in range(DEG - 1):
        remainder = remainder - operate(update, diagonal, fluid)
        rho_new = 1.0 / (2.0 * sigma_val - rho_old)
        update = rho_new * rho_old * update + 2.0 * rho_new / half_width * jacobi * remainder
        smooth = smooth + update
        rho_old = rho_new
    return smooth


def on_device(
    right_side, diagonal, solid_mask, geneo_vectors, vector_counts, owner_slots, coarse_inverse
):
    fluid = 1.0 - solid_mask.astype(jnp.float32)
    jacobi = 1.0 / (fluid * (6.0 + diagonal) + 1.0 - fluid)
    kcount = geneo_vectors.shape[0]
    shape_cells = right_side.shape
    live = (jnp.arange(kcount, dtype=jnp.int32) < vector_counts[0, 0]).astype(jnp.float32)
    vec_matrix = geneo_vectors.reshape(kcount, -1).astype(jnp.float32) * live[:, None]
    row_count = coarse_inverse.shape[0]
    block_len = coarse_inverse.shape[1]
    size_gy = lax.axis_size("gy")
    index_gx = lax.axis_index("gx")
    index_gy = lax.axis_index("gy")
    my_sub = index_gx * size_gy + index_gy
    my_slot = lax.dynamic_slice_in_dim(owner_slots, my_sub, 1, 0)[0]

    def precondition(res):
        smooth = smoother(res, diagonal, fluid, jacobi)
        projected = jnp.dot(vec_matrix, res.reshape(-1), precision=HIGH)
        every_rhs = lax.all_gather(projected[None, :], ("gx", "gy"), axis=0, tiled=True)
        ordered = jnp.zeros(every_rhs.shape, jnp.float32).at[owner_slots].set(every_rhs)
        ordered_blocks = ordered.reshape(-1, block_len)
        first_row = index_gy * row_count
        row_ids = first_row + jnp.arange(row_count, dtype=jnp.int32)
        picked = ordered_blocks[row_ids // block_len]
        coarse_part = jnp.sum(coarse_inverse * picked, axis=1)
        coarse_full = lax.all_gather(coarse_part, "gy", axis=0, tiled=True)
        coeffs = lax.dynamic_slice_in_dim(coarse_full.reshape(-1, kcount), my_slot, 1, 0)[0] * live
        fine = jnp.dot(coeffs, vec_matrix, precision=HIGH)
        inner = None
        return (smooth + fine.reshape(shape_cells), inner)

    def products(resid, pre, pre_image):
        return lax.psum((jnp.sum(resid * pre), jnp.sum(pre * pre_image)), ("gx", "gy"))

    solution = jnp.zeros_like(right_side)
    residual = right_side
    precond, inner = precondition(residual)
    image_pre = operate(precond, diagonal, fluid)
    norm_now, curvature = products(residual, precond, image_pre)
    step_len = norm_now / curvature
    direction = precond
    along = image_pre
    for repeat in range(ITERS):
        solution = solution + step_len * direction
        residual = residual - step_len * along
        if repeat + 1 < ITERS:
            precond, inner = precondition(residual)
            image_pre = operate(precond, diagonal, fluid)
            norm_next, curvature = products(residual, precond, image_pre)
            ratio_val = norm_next / norm_now
            step_len = norm_next / (curvature - ratio_val * norm_next / step_len)
            direction = precond + ratio_val * direction
            along = image_pre + ratio_val * along
            norm_now = norm_next
    return (solution, residual)


def solution(mesh):
    in_specs = (
        P("gx", "gy", None),
        P("gx", "gy", None),
        P("gx", "gy", None),
        P(None, "gx", "gy", None),
        P("gx", "gy"),
        P(),
        P("gy", None),
    )
    out_specs = (P("gx", "gy", None), P("gx", "gy", None))
    return jax.shard_map(
        on_device, mesh=mesh, in_specs=in_specs, out_specs=out_specs, check_vma=False
    )
```

profile of v0, /device:TPU:0, one launch (start us, length us, event | category | flops | bytes accessed | tf_op | source)
XLA Modules:
  0.0 304.8 jit_solution(2894546075494403240)
XLA Ops:
  3.0 5.6 %collective-permute-start.1 = (f32[1,16,128]{2,1,0:T(8,128)S(1)}, f32[1,16,128]{2,1,0:T(8,128)S(1)}, u32[]{:S(2)}, u32[]{:S(2)}) collective-permute-start(f32[1,16,128]{2,1,0:T(8,128)S(1)} %get-tuple-element.40), channel_id=1, source_target_pairs={{0,8},{8,16},{16,24},{1,9},{9,17},{17,25},{2,10},{10,18},{18,26},{... | collective-permute-start | bytes 24584 | tf_op jit(solution)/shard_map/ppermute | solution.py:21
  10.9 2.5 fusion
  13.5 2.8 fusion.9
  19.5 43.7 %all-reduce.6 = f32[1024]{0:T(1024)S(1)} all-reduce(f32[1024]{0:T(1024)S(1)} %dynamic-update-slice), channel_id=2, replica_groups=mesh['gx'=4,'gy'=8] {'gx','gy'}, use_global_device_ids=true, to_apply=%add.6 | all-reduce | flops 1024 | bytes 8192
  66.1 4.5 %collective-permute-start.5 = (f32[1,16,128]{2,1,0:T(8,128)S(1)}, f32[1,16,128]{2,1,0:T(8,128)S(1)}, u32[]{:S(2)}, u32[]{:S(2)}) collective-permute-start(f32[1,16,128]{2,1,0:T(8,128)S(1)} %get-tuple-element.38), channel_id=1, source_target_pairs={{0,8},{8,16},{16,24},{1,9},{9,17},{17,25},{2,10},{10,18},{18,26},{... | collective-permute-start | bytes 24584 | tf_op jit(solution)/shard_map/ppermute | solution.py:21
  72.8 3.3 %copy.24 = f32[4,8,128,128]{3,2,1,0:T(8,128)} copy(f32[4,8,128,128]{3,1,2,0:T(8,128)} %fusion) | data formatting | bytes 4194304
  76.1 9.5 %all-gather.2 = f32[8,1,128]{2,1,0:T(1,128)S(1)} all-gather(f32[1,1,128]{2,1,0:T(1,128)S(1)} %bitcast.64), channel_id=1, replica_groups=mesh['gx'=4,'gy'=8] {'gy'}, dimensions={0}, use_global_device_ids=true | all-gather | bytes 4608 | tf_op jit(solution)/shard_map/all_gather | solution.py:83
  87.6 2.2 collective-permute-start.7
  91.1 3.8 %fusion.3 = f32[1,8,16,128]{3,0,2,1:T(1,128)S(1)} fusion(f32[8,16,128,32]{2,1,0,3:T(8,128)} %bitcast.57, f32[32,32]{1,0:T(8,128)S(1)} %reshape.114, s32[]{:T(128)S(6)} %select_n.39, s32[]{:T(128)} %bitcast.54), kind=kOutput, calls=%fused_computation.8 | convolution fusion | flops 6291520 | bytes 2163208 | tf_op jit(solution)/shard_map/dot_general | solution.py:85
  96.4 4.5 %collective-permute-start.9 = (f32[1,16,128]{2,1,0:T(8,128)S(1)}, f32[1,16,128]{2,1,0:T(8,128)S(1)}, u32[]{:S(2)}, u32[]{:S(2)}) collective-permute-start(f32[1,16,128]{2,1,0:T(8,128)S(1)} %get-tuple-element.36), channel_id=1, source_target_pairs={{0,8},{8,16},{16,24},{1,9},{9,17},{17,25},{2,10},{10,18},{18,26},{... | collective-permute-start | bytes 24584 | tf_op jit(solution)/shard_map/ppermute | solution.py:21
  102.4 2.6 collective-permute-start.11
  106.3 4.1 %collective-permute-done.10 = f32[10,1,128]{2,1,0:T(1,128)S(1)} collective-permute-done((f32[10,1,128]{2,1,0:T(1,128)S(1)}, f32[10,1,128]{2,1,0:T(1,128)S(1)}, u32[]{:S(2)}, u32[]{:S(2)}) %collective-permute-start.10) | collective-permute-done | bytes 5152 | tf_op jit(solution)/shard_map/ppermute | solution.py:23
  111.2 43.8 %all-reduce.9 = (f32[]{:T(128)}, f32[]{:T(128)}) all-reduce(f32[]{:T(128)} %get-tuple-element.5, f32[]{:T(128)} %get-tuple-element.4), channel_id=1, replica_groups=mesh['gx'=4,'gy'=8] {'gx','gy'}, use_global_device_ids=true, to_apply=%region_3.4 | all-reduce | flops 2 | bytes 16 | tf_op jit(solution)/shard_map/psum | solution.py:90
  157.7 4.5 %collective-permute-start.13 = (f32[1,16,128]{2,1,0:T(8,128)S(1)}, f32[1,16,128]{2,1,0:T(8,128)S(1)}, u32[]{:S(2)}, u32[]{:S(2)}) collective-permute-start(f32[1,16,128]{2,1,0:T(8,128)S(1)} %get-tuple-element.34), channel_id=1, source_target_pairs={{0,8},{8,16},{16,24},{1,9},{9,17},{17,25},{2,10},{10,18},{18,26},{... | collective-permute-start | bytes 24584 | tf_op jit(solution)/shard_map/ppermute | solution.py:21
  166.4 2.8 fusion.12
  169.3 44.4 %all-reduce.7 = f32[1024]{0:T(1024)S(1)} all-reduce(f32[1024]{0:T(1024)S(1)} %dynamic-update-slice.1), channel_id=3, replica_groups=mesh['gx'=4,'gy'=8] {'gx','gy'}, use_global_device_ids=true, to_apply=%add.7 | all-reduce | flops 1024 | bytes 8192
  216.7 4.5 %collective-permute-start.17 = (f32[1,16,128]{2,1,0:T(8,128)S(1)}, f32[1,16,128]{2,1,0:T(8,128)S(1)}, u32[]{:S(2)}, u32[]{:S(2)}) collective-permute-start(f32[1,16,128]{2,1,0:T(8,128)S(1)} %get-tuple-element.32), channel_id=1, source_target_pairs={{0,8},{8,16},{16,24},{1,9},{9,17},{17,25},{2,10},{10,18},{18,26},{... | collective-permute-start | bytes 24584 | tf_op jit(solution)/shard_map/ppermute | solution.py:21
  221.3 9.6 %all-gather.3 = f32[8,1,128]{2,1,0:T(1,128)S(1)} all-gather(f32[1,1,128]{2,1,0:T(1,128)S(1)} %bitcast.65), channel_id=1, replica_groups=mesh['gx'=4,'gy'=8] {'gy'}, dimensions={0}, use_global_device_ids=true | all-gather | bytes 4608 | tf_op jit(solution)/shard_map/all_gather | solution.py:83
  231.6 2.2 collective-permute-start.19
  235.2 3.8 %fusion.1 = f32[1,8,16,128]{3,0,2,1:T(1,128)S(1)} fusion(f32[8,16,128,32]{2,1,0,3:T(8,128)} %bitcast.58, f32[32,32]{1,0:T(8,128)S(1)} %reshape.116, s32[]{:T(128)S(6)} %select_n.39, s32[]{:T(128)} %bitcast.56), kind=kOutput, calls=%fused_computation.6 | convolution fusion | flops 6291520 | bytes 2163208 | tf_op jit(solution)/shard_map/dot_general | solution.py:85
  240.5 4.5 %collective-permute-start.21 = (f32[1,16,128]{2,1,0:T(8,128)S(1)}, f32[1,16,128]{2,1,0:T(8,128)S(1)}, u32[]{:S(2)}, u32[]{:S(2)}) collective-permute-start(f32[1,16,128]{2,1,0:T(8,128)S(1)} %get-tuple-element.30), channel_id=1, source_target_pairs={{0,8},{8,16},{16,24},{1,9},{9,17},{17,25},{2,10},{10,18},{18,26},{... | collective-permute-start | bytes 24584 | tf_op jit(solution)/shard_map/ppermute | solution.py:21
  246.4 3.1 %collective-permute-start.23 = (f32[10,1,128]{2,1,0:T(1,128)S(1)}, f32[10,1,128]{2,1,0:T(1,128)S(1)}, u32[]{:S(2)}, u32[]{:S(2)}) collective-permute-start(f32[10,1,128]{2,1,0:T(1,128)S(1)} %get-tuple-element.19), channel_id=1, source_target_pairs={{0,1},{1,2},{2,3},{3,4},{4,5},{5,6},{6,7},{8,9},{9,10},{10,11},{11... | collective-permute-start | bytes 15368 | tf_op jit(solution)/shard_map/ppermute | solution.py:21
  250.8 4.1 %collective-permute-done.22 = f32[10,1,128]{2,1,0:T(1,128)S(1)} collective-permute-done((f32[10,1,128]{2,1,0:T(1,128)S(1)}, f32[10,1,128]{2,1,0:T(1,128)S(1)}, u32[]{:S(2)}, u32[]{:S(2)}) %collective-permute-start.22) | collective-permute-done | bytes 5152 | tf_op jit(solution)/shard_map/ppermute | solution.py:23
  255.7 43.8 %all-reduce.8 = (f32[]{:T(128)}, f32[]{:T(128)}) all-reduce(f32[]{:T(128)} %get-tuple-element.3, f32[]{:T(128)} %get-tuple-element.2), channel_id=1, replica_groups=mesh['gx'=4,'gy'=8] {'gx','gy'}, use_global_device_ids=true, to_apply=%region_9.10 | all-reduce | flops 2 | bytes 16 | tf_op jit(solution)/shard_map/psum | solution.py:90
  (96 shorter events, 34.4 us)
Async XLA Ops:
  1.7 14.6 %collective-permute-start = (f32[1,16,128]{2,1,0:T(8,128)S(1)}, f32[1,16,128]{2,1,0:T(8,128)S(1)}, u32[]{:S(2)}, u32[]{:S(2)}) collective-permute-start(f32[1,16,128]{2,1,0:T(8,128)S(1)} %get-tuple-element.41), channel_id=1, source_target_pairs={{8,0},{16,8},{24,16},{9,1},{17,9},{25,17},{10,2},{18,10},{26,18},{... | collective-permute-start | bytes 24584 | tf_op jit(solution)/shard_map/ppermute | solution.py:23
  3.0 13.3 %collective-permute-start.1 = (f32[1,16,128]{2,1,0:T(8,128)S(1)}, f32[1,16,128]{2,1,0:T(8,128)S(1)}, u32[]{:S(2)}, u32[]{:S(2)}) collective-permute-start(f32[1,16,128]{2,1,0:T(8,128)S(1)} %get-tuple-element.40), channel_id=1, source_target_pairs={{0,8},{8,16},{16,24},{1,9},{9,17},{17,25},{2,10},{10,18},{18,26},{... | collective-permute-start | bytes 24584 | tf_op jit(solution)/shard_map/ppermute | solution.py:21
  16.3 48.3 %collective-permute-start.3 = (f32[10,1,128]{2,1,0:T(1,128)S(1)}, f32[10,1,128]{2,1,0:T(1,128)S(1)}, u32[]{:S(2)}, u32[]{:S(2)}) collective-permute-start(f32[10,1,128]{2,1,0:T(1,128)S(1)} %get-tuple-element.29), channel_id=1, source_target_pairs={{0,1},{1,2},{2,3},{3,4},{4,5},{5,6},{6,7},{8,9},{9,10},{10,11},{11... | collective-permute-start | bytes 15368 | tf_op jit(solution)/shard_map/ppermute | solution.py:21
  17.8 46.8 %collective-permute-start.2 = (f32[10,1,128]{2,1,0:T(1,128)S(1)}, f32[10,1,128]{2,1,0:T(1,128)S(1)}, u32[]{:S(2)}, u32[]{:S(2)}) collective-permute-start(f32[10,1,128]{2,1,0:T(1,128)S(1)} %get-tuple-element.28), channel_id=1, source_target_pairs={{1,0},{2,1},{3,2},{4,3},{5,4},{6,5},{7,6},{9,8},{10,9},{11,10},{12... | collective-permute-start | bytes 15368 | tf_op jit(solution)/shard_map/ppermute | solution.py:23
  64.8 22.7 %collective-permute-start.4 = (f32[1,16,128]{2,1,0:T(8,128)S(1)}, f32[1,16,128]{2,1,0:T(8,128)S(1)}, u32[]{:S(2)}, u32[]{:S(2)}) collective-permute-start(f32[1,16,128]{2,1,0:T(8,128)S(1)} %get-tuple-element.39), channel_id=1, source_target_pairs={{8,0},{16,8},{24,16},{9,1},{17,9},{25,17},{10,2},{18,10},{26,18},{... | collective-permute-start | bytes 24584 | tf_op jit(solution)/shard_map/ppermute | solution.py:23
  66.1 21.5 %collective-permute-start.5 = (f32[1,16,128]{2,1,0:T(8,128)S(1)}, f32[1,16,128]{2,1,0:T(8,128)S(1)}, u32[]{:S(2)}, u32[]{:S(2)}) collective-permute-start(f32[1,16,128]{2,1,0:T(8,128)S(1)} %get-tuple-element.38), channel_id=1, source_target_pairs={{0,8},{8,16},{16,24},{1,9},{9,17},{17,25},{2,10},{10,18},{18,26},{... | collective-permute-start | bytes 24584 | tf_op jit(solution)/shard_map/ppermute | solution.py:21
  87.6 7.3 %collective-permute-start.7 = (f32[10,1,128]{2,1,0:T(1,128)S(1)}, f32[10,1,128]{2,1,0:T(1,128)S(1)}, u32[]{:S(2)}, u32[]{:S(2)}) collective-permute-start(f32[10,1,128]{2,1,0:T(1,128)S(1)} %get-tuple-element.27), channel_id=1, source_target_pairs={{0,1},{1,2},{2,3},{3,4},{4,5},{5,6},{6,7},{8,9},{9,10},{10,11},{11... | collective-permute-start | bytes 15368 | tf_op jit(solution)/shard_map/ppermute | solution.py:21
  89.8 5.1 %collective-permute-start.6 = (f32[10,1,128]{2,1,0:T(1,128)S(1)}, f32[10,1,128]{2,1,0:T(1,128)S(1)}, u32[]{:S(2)}, u32[]{:S(2)}) collective-permute-start(f32[10,1,128]{2,1,0:T(1,128)S(1)} %get-tuple-element.26), channel_id=1, source_target_pairs={{1,0},{2,1},{3,2},{4,3},{5,4},{6,5},{7,6},{9,8},{10,9},{11,10},{12... | collective-permute-start | bytes 15368 | tf_op jit(solution)/shard_map/ppermute | solution.py:23
  95.1 5.9 %collective-permute-start.8 = (f32[1,16,128]{2,1,0:T(8,128)S(1)}, f32[1,16,128]{2,1,0:T(8,128)S(1)}, u32[]{:S(2)}, u32[]{:S(2)}) collective-permute-start(f32[1,16,128]{2,1,0:T(8,128)S(1)} %get-tuple-element.37), channel_id=1, source_target_pairs={{8,0},{16,8},{24,16},{9,1},{17,9},{25,17},{10,2},{18,10},{26,18},{... | collective-permute-start | bytes 24584 | tf_op jit(solution)/shard_map/ppermute | solution.py:23
  96.4 5.9 %collective-permute-start.9 = (f32[1,16,128]{2,1,0:T(8,128)S(1)}, f32[1,16,128]{2,1,0:T(8,128)S(1)}, u32[]{:S(2)}, u32[]{:S(2)}) collective-permute-start(f32[1,16,128]{2,1,0:T(8,128)S(1)} %get-tuple-element.36), channel_id=1, source_target_pairs={{0,8},{8,16},{16,24},{1,9},{9,17},{17,25},{2,10},{10,18},{18,26},{... | collective-permute-start | bytes 24584 | tf_op jit(solution)/shard_map/ppermute | solution.py:21
  102.4 3.9 %collective-permute-start.11 = (f32[10,1,128]{2,1,0:T(1,128)S(1)}, f32[10,1,128]{2,1,0:T(1,128)S(1)}, u32[]{:S(2)}, u32[]{:S(2)}) collective-permute-start(f32[10,1,128]{2,1,0:T(1,128)S(1)} %get-tuple-element.25), channel_id=1, source_target_pairs={{0,1},{1,2},{2,3},{3,4},{4,5},{5,6},{6,7},{8,9},{9,10},{10,11},{11... | collective-permute-start | bytes 15368 | tf_op jit(solution)/shard_map/ppermute | solution.py:21
  105.0 5.4 %collective-permute-start.10 = (f32[10,1,128]{2,1,0:T(1,128)S(1)}, f32[10,1,128]{2,1,0:T(1,128)S(1)}, u32[]{:S(2)}, u32[]{:S(2)}) collective-permute-start(f32[10,1,128]{2,1,0:T(1,128)S(1)} %get-tuple-element.24), channel_id=1, source_target_pairs={{1,0},{2,1},{3,2},{4,3},{5,4},{6,5},{7,6},{9,8},{10,9},{11,10},{12... | collective-permute-start | bytes 15368 | tf_op jit(solution)/shard_map/ppermute | solution.py:23
  156.4 5.9 %collective-permute-start.12 = (f32[1,16,128]{2,1,0:T(8,128)S(1)}, f32[1,16,128]{2,1,0:T(8,128)S(1)}, u32[]{:S(2)}, u32[]{:S(2)}) collective-permute-start(f32[1,16,128]{2,1,0:T(8,128)S(1)} %get-tuple-element.35), channel_id=1, source_target_pairs={{8,0},{16,8},{24,16},{9,1},{17,9},{25,17},{10,2},{18,10},{26,18},{... | collective-permute-start | bytes 24584 | tf_op jit(solution)/shard_map/ppermute | solution.py:23
  157.7 5.9 %collective-permute-start.13 = (f32[1,16,128]{2,1,0:T(8,128)S(1)}, f32[1,16,128]{2,1,0:T(8,128)S(1)}, u32[]{:S(2)}, u32[]{:S(2)}) collective-permute-start(f32[1,16,128]{2,1,0:T(8,128)S(1)} %get-tuple-element.34), channel_id=1, source_target_pairs={{0,8},{8,16},{16,24},{1,9},{9,17},{17,25},{2,10},{10,18},{18,26},{... | collective-permute-start | bytes 24584 | tf_op jit(solution)/shard_map/ppermute | solution.py:21
  163.6 51.6 %collective-permute-start.15 = (f32[10,1,128]{2,1,0:T(1,128)S(1)}, f32[10,1,128]{2,1,0:T(1,128)S(1)}, u32[]{:S(2)}, u32[]{:S(2)}) collective-permute-start(f32[10,1,128]{2,1,0:T(1,128)S(1)} %get-tuple-element.23), channel_id=1, source_target_pairs={{0,1},{1,2},{2,3},{3,4},{4,5},{5,6},{6,7},{8,9},{9,10},{10,11},{11... | collective-permute-start | bytes 15368 | tf_op jit(solution)/shard_map/ppermute | solution.py:21
  164.9 50.3 %collective-permute-start.14 = (f32[10,1,128]{2,1,0:T(1,128)S(1)}, f32[10,1,128]{2,1,0:T(1,128)S(1)}, u32[]{:S(2)}, u32[]{:S(2)}) collective-permute-start(f32[10,1,128]{2,1,0:T(1,128)S(1)} %get-tuple-element.22), channel_id=1, source_target_pairs={{1,0},{2,1},{3,2},{4,3},{5,4},{6,5},{7,6},{9,8},{10,9},{11,10},{12... | collective-permute-start | bytes 15368 | tf_op jit(solution)/shard_map/ppermute | solution.py:23
  215.4 16.3 %collective-permute-start.16 = (f32[1,16,128]{2,1,0:T(8,128)S(1)}, f32[1,16,128]{2,1,0:T(8,128)S(1)}, u32[]{:S(2)}, u32[]{:S(2)}) collective-permute-start(f32[1,16,128]{2,1,0:T(8,128)S(1)} %get-tuple-element.33), channel_id=1, source_target_pairs={{8,0},{16,8},{24,16},{9,1},{17,9},{25,17},{10,2},{18,10},{26,18},{... | collective-permute-start | bytes 24584 | tf_op jit(solution)/shard_map/ppermute | solution.py:23
  216.7 15.0 %collective-permute-start.17 = (f32[1,16,128]{2,1,0:T(8,128)S(1)}, f32[1,16,128]{2,1,0:T(8,128)S(1)}, u32[]{:S(2)}, u32[]{:S(2)}) collective-permute-start(f32[1,16,128]{2,1,0:T(8,128)S(1)} %get-tuple-element.32), channel_id=1, source_target_pairs={{0,8},{8,16},{16,24},{1,9},{9,17},{17,25},{2,10},{10,18},{18,26},{... | collective-permute-start | bytes 24584 | tf_op jit(solution)/shard_map/ppermute | solution.py:21
  231.6 7.3 %collective-permute-start.19 = (f32[10,1,128]{2,1,0:T(1,128)S(1)}, f32[10,1,128]{2,1,0:T(1,128)S(1)}, u32[]{:S(2)}, u32[]{:S(2)}) collective-permute-start(f32[10,1,128]{2,1,0:T(1,128)S(1)} %get-tuple-element.21), channel_id=1, source_target_pairs={{0,1},{1,2},{2,3},{3,4},{4,5},{5,6},{6,7},{8,9},{9,10},{10,11},{11... | collective-permute-start | bytes 15368 | tf_op jit(solution)/shard_map/ppermute | solution.py:21
  233.9 5.1 %collective-permute-start.18 = (f32[10,1,128]{2,1,0:T(1,128)S(1)}, f32[10,1,128]{2,1,0:T(1,128)S(1)}, u32[]{:S(2)}, u32[]{:S(2)}) collective-permute-start(f32[10,1,128]{2,1,0:T(1,128)S(1)} %get-tuple-element.20), channel_id=1, source_target_pairs={{1,0},{2,1},{3,2},{4,3},{5,4},{6,5},{7,6},{9,8},{10,9},{11,10},{12... | collective-permute-start | bytes 15368 | tf_op jit(solution)/shard_map/ppermute | solution.py:23
  239.2 5.9 %collective-permute-start.20 = (f32[1,16,128]{2,1,0:T(8,128)S(1)}, f32[1,16,128]{2,1,0:T(8,128)S(1)}, u32[]{:S(2)}, u32[]{:S(2)}) collective-permute-start(f32[1,16,128]{2,1,0:T(8,128)S(1)} %get-tuple-element.31), channel_id=1, source_target_pairs={{8,0},{16,8},{24,16},{9,1},{17,9},{25,17},{10,2},{18,10},{26,18},{... | collective-permute-start | bytes 24584 | tf_op jit(solution)/shard_map/ppermute | solution.py:23
  240.5 5.9 %collective-permute-start.21 = (f32[1,16,128]{2,1,0:T(8,128)S(1)}, f32[1,16,128]{2,1,0:T(8,128)S(1)}, u32[]{:S(2)}, u32[]{:S(2)}) collective-permute-start(f32[1,16,128]{2,1,0:T(8,128)S(1)} %get-tuple-element.30), channel_id=1, source_target_pairs={{0,8},{8,16},{16,24},{1,9},{9,17},{17,25},{2,10},{10,18},{18,26},{... | collective-permute-start | bytes 24584 | tf_op jit(solution)/shard_map/ppermute | solution.py:21
  246.4 4.4 %collective-permute-start.23 = (f32[10,1,128]{2,1,0:T(1,128)S(1)}, f32[10,1,128]{2,1,0:T(1,128)S(1)}, u32[]{:S(2)}, u32[]{:S(2)}) collective-permute-start(f32[10,1,128]{2,1,0:T(1,128)S(1)} %get-tuple-element.19), channel_id=1, source_target_pairs={{0,1},{1,2},{2,3},{3,4},{4,5},{5,6},{6,7},{8,9},{9,10},{10,11},{11... | collective-permute-start | bytes 15368 | tf_op jit(solution)/shard_map/ppermute | solution.py:21
  249.5 5.4 %collective-permute-start.22 = (f32[10,1,128]{2,1,0:T(1,128)S(1)}, f32[10,1,128]{2,1,0:T(1,128)S(1)}, u32[]{:S(2)}, u32[]{:S(2)}) collective-permute-start(f32[10,1,128]{2,1,0:T(1,128)S(1)} %get-tuple-element.18), channel_id=1, source_target_pairs={{1,0},{2,1},{3,2},{4,3},{5,4},{6,5},{7,6},{9,8},{10,9},{11,10},{12... | collective-permute-start | bytes 15368 | tf_op jit(solution)/shard_map/ppermute | solution.py:23
  (6 other events, 123.2 us)
where the time goes:
time: 306 us; the launch traced here: 305 us
  blocking collectives  195 us (64%)
  starting transfers between devices  57 us (19%)
  matrix products  13 us (4%)
  waiting for transfers between devices  12.3 us (4%)
  between operations  10 us (3%)
  other arithmetic  9.63 us (3%)
  local copies, waits for them, and re-layouts  8.08 us (3%)
    unnamed x2, blocking collectives  88.1 us
    psum x2, blocking collectives, products(): lax.psum((jnp.sum(resid * pre), jnp.sum(pre * pre_image)), ('gx', 'gy'))  87.6 us
    ppermute x12, starting transfers between devices, with_halo(): lax.ppermute(tail, axis, [(i, (i + 1) % count) for i in range(ends)])  41.3 us
    all_gather x2, blocking collectives, precondition(): coarse_full = lax.all_gather(coarse_part, 'gy', axis=0, tiled=True)  19.1 us
    ppermute x12, starting transfers between devices, with_halo(): lax.ppermute(head, axis, [((i + 1) % count, i) for i in range(ends)])  15.7 us
    ppermute x12, waiting for transfers between devices, with_halo(): lax.ppermute(head, axis, [((i + 1) % count, i) for i in range(ends)])  8.28 us
    dot_general x2, matrix products, precondition(): fine = jnp.dot(coeffs, vec_matrix, precision=HIGH)  7.52 us
  transfers between devices with their start and end apart: 24, of which 5 were waited for; matrix products, arithmetic and copies ran while one was open for 9% of the time, Pallas kernels for 0%

commit v1 on v0

--- a/solution.py
+++ b/solution.py
@@ -87,7 +87,7 @@
         return (smooth + fine.reshape(shape_cells), inner)
 
     def products(resid, pre, pre_image):
-        return lax.psum((jnp.sum(resid * pre), jnp.sum(pre * pre_image)), ("gx", "gy"))
+        return lax.psum(lax.psum((jnp.sum(resid * pre), jnp.sum(pre * pre_image)), "gy"), "gx")
 
     solution = jnp.zeros_like(right_side)
     residual = right_side

time: 306 us -> 274 us (0.90)
  blocking collectives: 195 us -> 162 us
    psum x2 -> x4, blocking collectives: 87.6 us -> 53.2 us  [the longest x2 30.4 us: products(): lax.psum((jnp.sum(resid * pre), jnp.sum(pre * pre_image)), 'gy')]
  transfers between devices with their start and end apart: 24 -> 24, of which waited for: 5 -> 5; matrix products, arithmetic and copies ran while one was open for 9% -> 10% of each run, Pallas kernels for 0% -> 0%
where the time goes in v1:
time: 274 us; the launch traced here: 271 us
  blocking collectives  162 us (59%)
  starting transfers between devices  57 us (21%)
  matrix products  13 us (5%)
  waiting for transfers between devices  12.3 us (4%)
  other arithmetic  9.66 us (4%)
  between operations  9.63 us (4%)
  local copies, waits for them, and re-layouts  8.04 us (3%)
    unnamed x2, blocking collectives  89.5 us
    ppermute x12, starting transfers between devices, with_halo(): lax.ppermute(tail, axis, [(i, (i + 1) % count) for i in range(ends)])  41.3 us
    psum x2, blocking collectives, products(): lax.psum((jnp.sum(resid * pre), jnp.sum(pre * pre_image)), 'gy')  30.4 us
    psum x2, blocking collectives, products(): lax.psum(lax.psum((jnp.sum(resid * pre), jnp.sum(pre * pre_image)), 'gy')...  22.7 us
    all_gather x2, blocking collectives, precondition(): coarse_full = lax.all_gather(coarse_part, 'gy', axis=0, tiled=True)  19.1 us
    ppermute x12, starting transfers between devices, with_halo(): lax.ppermute(head, axis, [((i + 1) % count, i) for i in range(ends)])  15.7 us
    ppermute x12, waiting for transfers between devices, with_halo(): lax.ppermute(head, axis, [((i + 1) % count, i) for i in range(ends)])  8.28 us
    dot_general x2, matrix products, precondition(): fine = jnp.dot(coeffs, vec_matrix, precision=HIGH)  7.52 us
  transfers between devices with their start and end apart: 24, of which 5 were waited for; matrix products, arithmetic and copies ran while one was open for 10% of the time, Pallas kernels for 0%

profile of v1, /device:TPU:0, one launch (start us, length us, event | category | flops | bytes accessed | tf_op | source)
XLA Modules:
  0.0 271.4 jit_solution(9302777138392834874)
XLA Ops:
  3.0 5.6 %collective-permute-start.1 = (f32[1,16,128]{2,1,0:T(8,128)S(1)}, f32[1,16,128]{2,1,0:T(8,128)S(1)}, u32[]{:S(2)}, u32[]{:S(2)}) collective-permute-start(f32[1,16,128]{2,1,0:T(8,128)S(1)} %get-tuple-element.44), channel_id=1, source_target_pairs={{0,8},{8,16},{16,24},{1,9},{9,17},{17,25},{2,10},{10,18},{18,26},{... | collective-permute-start | bytes 24584 | tf_op jit(solution)/shard_map/ppermute | solution.py:21
  10.9 2.5 fusion
  13.5 2.8 %fusion.9 = f32[32]{0:T(128)S(1)} fusion(f32[8,16,128,1]{2,3,1,0:T(1,128)S(1)} %bitcast.60, f32[32,8,16,128]{3,2,1,0:T(8,128)S(1)} %broadcast_multiply_fusion), kind=kOutput, calls=%fused_computation.14 | convolution fusion | flops 6291456 | bytes 2162816 | tf_op jit(solution)/shard_map/dot_general | solution.py:75
  19.5 43.7 %all-reduce.6 = f32[1024]{0:T(1024)S(1)} all-reduce(f32[1024]{0:T(1024)S(1)} %dynamic-update-slice), channel_id=2, replica_groups=mesh['gx'=4,'gy'=8] {'gx','gy'}, use_global_device_ids=true, to_apply=%add.6 | all-reduce | flops 1024 | bytes 8192
  66.1 4.5 %collective-permute-start.5 = (f32[1,16,128]{2,1,0:T(8,128)S(1)}, f32[1,16,128]{2,1,0:T(8,128)S(1)}, u32[]{:S(2)}, u32[]{:S(2)}) collective-permute-start(f32[1,16,128]{2,1,0:T(8,128)S(1)} %get-tuple-element.42), channel_id=1, source_target_pairs={{0,8},{8,16},{16,24},{1,9},{9,17},{17,25},{2,10},{10,18},{18,26},{... | collective-permute-start | bytes 24584 | tf_op jit(solution)/shard_map/ppermute | solution.py:21
  72.6 3.3 %copy.24 = f32[4,8,128,128]{3,2,1,0:T(8,128)} copy(f32[4,8,128,128]{3,1,2,0:T(8,128)} %fusion) | data formatting | bytes 4194304
  75.9 9.5 %all-gather.2 = f32[8,1,128]{2,1,0:T(1,128)S(1)} all-gather(f32[1,1,128]{2,1,0:T(1,128)S(1)} %bitcast.64), channel_id=1, replica_groups=mesh['gx'=4,'gy'=8] {'gy'}, dimensions={0}, use_global_device_ids=true | all-gather | bytes 4608 | tf_op jit(solution)/shard_map/all_gather | solution.py:83
  90.9 3.8 %fusion.3 = f32[1,8,16,128]{3,0,2,1:T(1,128)S(1)} fusion(f32[8,16,128,32]{2,1,0,3:T(8,128)} %bitcast.57, f32[32,32]{1,0:T(8,128)S(1)} %reshape.114, s32[]{:T(128)S(6)} %select_n.39, s32[]{:T(128)} %bitcast.54), kind=kOutput, calls=%fused_computation.8 | convolution fusion | flops 6291520 | bytes 2163208 | tf_op jit(solution)/shard_map/dot_general | solution.py:85
  96.2 4.5 %collective-permute-start.9 = (f32[1,16,128]{2,1,0:T(8,128)S(1)}, f32[1,16,128]{2,1,0:T(8,128)S(1)}, u32[]{:S(2)}, u32[]{:S(2)}) collective-permute-start(f32[1,16,128]{2,1,0:T(8,128)S(1)} %get-tuple-element.40), channel_id=1, source_target_pairs={{0,8},{8,16},{16,24},{1,9},{9,17},{17,25},{2,10},{10,18},{18,26},{... | collective-permute-start | bytes 24584 | tf_op jit(solution)/shard_map/ppermute | solution.py:21
  102.1 2.6 collective-permute-start.11
  106.1 4.1 %collective-permute-done.10 = f32[10,1,128]{2,1,0:T(1,128)S(1)} collective-permute-done((f32[10,1,128]{2,1,0:T(1,128)S(1)}, f32[10,1,128]{2,1,0:T(1,128)S(1)}, u32[]{:S(2)}, u32[]{:S(2)}) %collective-permute-start.10) | collective-permute-done | bytes 5152 | tf_op jit(solution)/shard_map/ppermute | solution.py:23
  111.0 15.3 %all-reduce.9 = (f32[]{:T(128)}, f32[]{:T(128)}) all-reduce(f32[]{:T(128)} %get-tuple-element.5, f32[]{:T(128)} %get-tuple-element.4), channel_id=1, replica_groups=mesh['gx'=4,'gy'=8] {'gy'}, use_global_device_ids=true, to_apply=%region_3.4 | all-reduce | flops 2 | bytes 16 | tf_op jit(solution)/shard_map/psum | solution.py:90
  126.2 11.5 %all-reduce.11 = (f32[]{:T(128)}, f32[]{:T(128)}) all-reduce(f32[]{:T(128)} %get-tuple-element.8, f32[]{:T(128)} %get-tuple-element.9), channel_id=1, replica_groups=mesh['gx'=4,'gy'=8] {'gx'}, use_global_device_ids=true, to_apply=%region_4.5 | all-reduce | flops 2 | bytes 16 | tf_op jit(solution)/shard_map/psum | solution.py:90
  140.4 4.5 %collective-permute-start.13 = (f32[1,16,128]{2,1,0:T(8,128)S(1)}, f32[1,16,128]{2,1,0:T(8,128)S(1)}, u32[]{:S(2)}, u32[]{:S(2)}) collective-permute-start(f32[1,16,128]{2,1,0:T(8,128)S(1)} %get-tuple-element.38), channel_id=1, source_target_pairs={{0,8},{8,16},{16,24},{1,9},{9,17},{17,25},{2,10},{10,18},{18,26},{... | collective-permute-start | bytes 24584 | tf_op jit(solution)/shard_map/ppermute | solution.py:21
  149.1 2.8 %fusion.12 = f32[32]{0:T(128)S(1)} fusion(f32[8,16,128,1]{2,3,1,0:T(1,128)S(1)} %bitcast.61, f32[32,8,16,128]{3,2,1,0:T(8,128)S(1)} %broadcast_multiply_fusion), kind=kOutput, calls=%fused_computation.15 | convolution fusion | flops 6291456 | bytes 2162816 | tf_op jit(solution)/shard_map/dot_general | solution.py:75
  152.0 45.8 %all-reduce.7 = f32[1024]{0:T(1024)S(1)} all-reduce(f32[1024]{0:T(1024)S(1)} %dynamic-update-slice.1), channel_id=3, replica_groups=mesh['gx'=4,'gy'=8] {'gx','gy'}, use_global_device_ids=true, to_apply=%add.7 | all-reduce | flops 1024 | bytes 8192
  200.7 4.5 %collective-permute-start.17 = (f32[1,16,128]{2,1,0:T(8,128)S(1)}, f32[1,16,128]{2,1,0:T(8,128)S(1)}, u32[]{:S(2)}, u32[]{:S(2)}) collective-permute-start(f32[1,16,128]{2,1,0:T(8,128)S(1)} %get-tuple-element.36), channel_id=1, source_target_pairs={{0,8},{8,16},{16,24},{1,9},{9,17},{17,25},{2,10},{10,18},{18,26},{... | collective-permute-start | bytes 24584 | tf_op jit(solution)/shard_map/ppermute | solution.py:21
  205.4 9.6 %all-gather.3 = f32[8,1,128]{2,1,0:T(1,128)S(1)} all-gather(f32[1,1,128]{2,1,0:T(1,128)S(1)} %bitcast.65), channel_id=1, replica_groups=mesh['gx'=4,'gy'=8] {'gy'}, dimensions={0}, use_global_device_ids=true | all-gather | bytes 4608 | tf_op jit(solution)/shard_map/all_gather | solution.py:83
  219.3 3.8 %fusion.1 = f32[1,8,16,128]{3,0,2,1:T(1,128)S(1)} fusion(f32[8,16,128,32]{2,1,0,3:T(8,128)} %bitcast.58, f32[32,32]{1,0:T(8,128)S(1)} %reshape.116, s32[]{:T(128)S(6)} %select_n.39, s32[]{:T(128)} %bitcast.56), kind=kOutput, calls=%fused_computation.6 | convolution fusion | flops 6291520 | bytes 2163208 | tf_op jit(solution)/shard_map/dot_general | solution.py:85
  224.6 4.5 %collective-permute-start.21 = (f32[1,16,128]{2,1,0:T(8,128)S(1)}, f32[1,16,128]{2,1,0:T(8,128)S(1)}, u32[]{:S(2)}, u32[]{:S(2)}) collective-permute-start(f32[1,16,128]{2,1,0:T(8,128)S(1)} %get-tuple-element.34), channel_id=1, source_target_pairs={{0,8},{8,16},{16,24},{1,9},{9,17},{17,25},{2,10},{10,18},{18,26},{... | collective-permute-start | bytes 24584 | tf_op jit(solution)/shard_map/ppermute | solution.py:21
  230.5 3.1 %collective-permute-start.23 = (f32[10,1,128]{2,1,0:T(1,128)S(1)}, f32[10,1,128]{2,1,0:T(1,128)S(1)}, u32[]{:S(2)}, u32[]{:S(2)}) collective-permute-start(f32[10,1,128]{2,1,0:T(1,128)S(1)} %get-tuple-element.23), channel_id=1, source_target_pairs={{0,1},{1,2},{2,3},{3,4},{4,5},{5,6},{6,7},{8,9},{9,10},{10,11},{11... | collective-permute-start | bytes 15368 | tf_op jit(solution)/shard_map/ppermute | solution.py:21
  234.9 4.1 %collective-permute-done.22 = f32[10,1,128]{2,1,0:T(1,128)S(1)} collective-permute-done((f32[10,1,128]{2,1,0:T(1,128)S(1)}, f32[10,1,128]{2,1,0:T(1,128)S(1)}, u32[]{:S(2)}, u32[]{:S(2)}) %collective-permute-start.22) | collective-permute-done | bytes 5152 | tf_op jit(solution)/shard_map/ppermute | solution.py:23
  239.8 15.2 %all-reduce.8 = (f32[]{:T(128)}, f32[]{:T(128)}) all-reduce(f32[]{:T(128)} %get-tuple-element.3, f32[]{:T(128)} %get-tuple-element.2), channel_id=1, replica_groups=mesh['gx'=4,'gy'=8] {'gy'}, use_global_device_ids=true, to_apply=%region_11.12 | all-reduce | flops 2 | bytes 16 | tf_op jit(solution)/shard_map/psum | solution.py:90
  254.9 11.3 %all-reduce.10 = (f32[]{:T(128)}, f32[]{:T(128)}) all-reduce(f32[]{:T(128)} %get-tuple-element.6, f32[]{:T(128)} %get-tuple-element.7), channel_id=1, replica_groups=mesh['gx'=4,'gy'=8] {'gx'}, use_global_device_ids=true, to_apply=%region_12.13 | all-reduce | flops 2 | bytes 16 | tf_op jit(solution)/shard_map/psum | solution.py:90
  (98 shorter events, 38.8 us)
Async XLA Ops:
  1.7 14.6 %collective-permute-start = (f32[1,16,128]{2,1,0:T(8,128)S(1)}, f32[1,16,128]{2,1,0:T(8,128)S(1)}, u32[]{:S(2)}, u32[]{:S(2)}) collective-permute-start(f32[1,16,128]{2,1,0:T(8,128)S(1)} %get-tuple-element.45), channel_id=1, source_target_pairs={{8,0},{16,8},{24,16},{9,1},{17,9},{25,17},{10,2},{18,10},{26,18},{... | collective-permute-start | bytes 24584 | tf_op jit(solution)/shard_map/ppermute | solution.py:23
  3.0 13.3 %collective-permute-start.1 = (f32[1,16,128]{2,1,0:T(8,128)S(1)}, f32[1,16,128]{2,1,0:T(8,128)S(1)}, u32[]{:S(2)}, u32[]{:S(2)}) collective-permute-start(f32[1,16,128]{2,1,0:T(8,128)S(1)} %get-tuple-element.44), channel_id=1, source_target_pairs={{0,8},{8,16},{16,24},{1,9},{9,17},{17,25},{2,10},{10,18},{18,26},{... | collective-permute-start | bytes 24584 | tf_op jit(solution)/shard_map/ppermute | solution.py:21
  16.3 48.3 %collective-permute-start.3 = (f32[10,1,128]{2,1,0:T(1,128)S(1)}, f32[10,1,128]{2,1,0:T(1,128)S(1)}, u32[]{:S(2)}, u32[]{:S(2)}) collective-permute-start(f32[10,1,128]{2,1,0:T(1,128)S(1)} %get-tuple-element.33), channel_id=1, source_target_pairs={{0,1},{1,2},{2,3},{3,4},{4,5},{5,6},{6,7},{8,9},{9,10},{10,11},{11... | collective-permute-start | bytes 15368 | tf_op jit(solution)/shard_map/ppermute | solution.py:21
  17.8 46.8 %collective-permute-start.2 = (f32[10,1,128]{2,1,0:T(1,128)S(1)}, f32[10,1,128]{2,1,0:T(1,128)S(1)}, u32[]{:S(2)}, u32[]{:S(2)}) collective-permute-start(f32[10,1,128]{2,1,0:T(1,128)S(1)} %get-tuple-element.32), channel_id=1, source_target_pairs={{1,0},{2,1},{3,2},{4,3},{5,4},{6,5},{7,6},{9,8},{10,9},{11,10},{12... | collective-permute-start | bytes 15368 | tf_op jit(solution)/shard_map/ppermute | solution.py:23
  64.8 22.5 %collective-permute-start.4 = (f32[1,16,128]{2,1,0:T(8,128)S(1)}, f32[1,16,128]{2,1,0:T(8,128)S(1)}, u32[]{:S(2)}, u32[]{:S(2)}) collective-permute-start(f32[1,16,128]{2,1,0:T(8,128)S(1)} %get-tuple-element.43), channel_id=1, source_target_pairs={{8,0},{16,8},{24,16},{9,1},{17,9},{25,17},{10,2},{18,10},{26,18},{... | collective-permute-start | bytes 24584 | tf_op jit(solution)/shard_map/ppermute | solution.py:23
  66.1 21.2 %collective-permute-start.5 = (f32[1,16,128]{2,1,0:T(8,128)S(1)}, f32[1,16,128]{2,1,0:T(8,128)S(1)}, u32[]{:S(2)}, u32[]{:S(2)}) collective-permute-start(f32[1,16,128]{2,1,0:T(8,128)S(1)} %get-tuple-element.42), channel_id=1, source_target_pairs={{0,8},{8,16},{16,24},{1,9},{9,17},{17,25},{2,10},{10,18},{18,26},{... | collective-permute-start | bytes 24584 | tf_op jit(solution)/shard_map/ppermute | solution.py:21
  87.4 7.3 %collective-permute-start.7 = (f32[10,1,128]{2,1,0:T(1,128)S(1)}, f32[10,1,128]{2,1,0:T(1,128)S(1)}, u32[]{:S(2)}, u32[]{:S(2)}) collective-permute-start(f32[10,1,128]{2,1,0:T(1,128)S(1)} %get-tuple-element.31), channel_id=1, source_target_pairs={{0,1},{1,2},{2,3},{3,4},{4,5},{5,6},{6,7},{8,9},{9,10},{10,11},{11... | collective-permute-start | bytes 15368 | tf_op jit(solution)/shard_map/ppermute | solution.py:21
  89.6 5.1 %collective-permute-start.6 = (f32[10,1,128]{2,1,0:T(1,128)S(1)}, f32[10,1,128]{2,1,0:T(1,128)S(1)}, u32[]{:S(2)}, u32[]{:S(2)}) collective-permute-start(f32[10,1,128]{2,1,0:T(1,128)S(1)} %get-tuple-element.30), channel_id=1, source_target_pairs={{1,0},{2,1},{3,2},{4,3},{5,4},{6,5},{7,6},{9,8},{10,9},{11,10},{12... | collective-permute-start | bytes 15368 | tf_op jit(solution)/shard_map/ppermute | solution.py:23
  94.9 5.9 %collective-permute-start.8 = (f32[1,16,128]{2,1,0:T(8,128)S(1)}, f32[1,16,128]{2,1,0:T(8,128)S(1)}, u32[]{:S(2)}, u32[]{:S(2)}) collective-permute-start(f32[1,16,128]{2,1,0:T(8,128)S(1)} %get-tuple-element.41), channel_id=1, source_target_pairs={{8,0},{16,8},{24,16},{9,1},{17,9},{25,17},{10,2},{18,10},{26,18},{... | collective-permute-start | bytes 24584 | tf_op jit(solution)/shard_map/ppermute | solution.py:23
  96.2 5.9 %collective-permute-start.9 = (f32[1,16,128]{2,1,0:T(8,128)S(1)}, f32[1,16,128]{2,1,0:T(8,128)S(1)}, u32[]{:S(2)}, u32[]{:S(2)}) collective-permute-start(f32[1,16,128]{2,1,0:T(8,128)S(1)} %get-tuple-element.40), channel_id=1, source_target_pairs={{0,8},{8,16},{16,24},{1,9},{9,17},{17,25},{2,10},{10,18},{18,26},{... | collective-permute-start | bytes 24584 | tf_op jit(solution)/shard_map/ppermute | solution.py:21
  102.1 3.9 %collective-permute-start.11 = (f32[10,1,128]{2,1,0:T(1,128)S(1)}, f32[10,1,128]{2,1,0:T(1,128)S(1)}, u32[]{:S(2)}, u32[]{:S(2)}) collective-permute-start(f32[10,1,128]{2,1,0:T(1,128)S(1)} %get-tuple-element.29), channel_id=1, source_target_pairs={{0,1},{1,2},{2,3},{3,4},{4,5},{5,6},{6,7},{8,9},{9,10},{10,11},{11... | collective-permute-start | bytes 15368 | tf_op jit(solution)/shard_map/ppermute | solution.py:21
  104.8 5.4 %collective-permute-start.10 = (f32[10,1,128]{2,1,0:T(1,128)S(1)}, f32[10,1,128]{2,1,0:T(1,128)S(1)}, u32[]{:S(2)}, u32[]{:S(2)}) collective-permute-start(f32[10,1,128]{2,1,0:T(1,128)S(1)} %get-tuple-element.28), channel_id=1, source_target_pairs={{1,0},{2,1},{3,2},{4,3},{5,4},{6,5},{7,6},{9,8},{10,9},{11,10},{12... | collective-permute-start | bytes 15368 | tf_op jit(solution)/shard_map/ppermute | solution.py:23
  139.1 5.9 %collective-permute-start.12 = (f32[1,16,128]{2,1,0:T(8,128)S(1)}, f32[1,16,128]{2,1,0:T(8,128)S(1)}, u32[]{:S(2)}, u32[]{:S(2)}) collective-permute-start(f32[1,16,128]{2,1,0:T(8,128)S(1)} %get-tuple-element.39), channel_id=1, source_target_pairs={{8,0},{16,8},{24,16},{9,1},{17,9},{25,17},{10,2},{18,10},{26,18},{... | collective-permute-start | bytes 24584 | tf_op jit(solution)/shard_map/ppermute | solution.py:23
  140.4 5.9 %collective-permute-start.13 = (f32[1,16,128]{2,1,0:T(8,128)S(1)}, f32[1,16,128]{2,1,0:T(8,128)S(1)}, u32[]{:S(2)}, u32[]{:S(2)}) collective-permute-start(f32[1,16,128]{2,1,0:T(8,128)S(1)} %get-tuple-element.38), channel_id=1, source_target_pairs={{0,8},{8,16},{16,24},{1,9},{9,17},{17,25},{2,10},{10,18},{18,26},{... | collective-permute-start | bytes 24584 | tf_op jit(solution)/shard_map/ppermute | solution.py:21
  146.3 53.0 %collective-permute-start.15 = (f32[10,1,128]{2,1,0:T(1,128)S(1)}, f32[10,1,128]{2,1,0:T(1,128)S(1)}, u32[]{:S(2)}, u32[]{:S(2)}) collective-permute-start(f32[10,1,128]{2,1,0:T(1,128)S(1)} %get-tuple-element.27), channel_id=1, source_target_pairs={{0,1},{1,2},{2,3},{3,4},{4,5},{5,6},{6,7},{8,9},{9,10},{10,11},{11... | collective-permute-start | bytes 15368 | tf_op jit(solution)/shard_map/ppermute | solution.py:21
  147.6 51.7 %collective-permute-start.14 = (f32[10,1,128]{2,1,0:T(1,128)S(1)}, f32[10,1,128]{2,1,0:T(1,128)S(1)}, u32[]{:S(2)}, u32[]{:S(2)}) collective-permute-start(f32[10,1,128]{2,1,0:T(1,128)S(1)} %get-tuple-element.26), channel_id=1, source_target_pairs={{1,0},{2,1},{3,2},{4,3},{5,4},{6,5},{7,6},{9,8},{10,9},{11,10},{12... | collective-permute-start | bytes 15368 | tf_op jit(solution)/shard_map/ppermute | solution.py:23
  199.4 16.3 %collective-permute-start.16 = (f32[1,16,128]{2,1,0:T(8,128)S(1)}, f32[1,16,128]{2,1,0:T(8,128)S(1)}, u32[]{:S(2)}, u32[]{:S(2)}) collective-permute-start(f32[1,16,128]{2,1,0:T(8,128)S(1)} %get-tuple-element.37), channel_id=1, source_target_pairs={{8,0},{16,8},{24,16},{9,1},{17,9},{25,17},{10,2},{18,10},{26,18},{... | collective-permute-start | bytes 24584 | tf_op jit(solution)/shard_map/ppermute | solution.py:23
  200.7 15.0 %collective-permute-start.17 = (f32[1,16,128]{2,1,0:T(8,128)S(1)}, f32[1,16,128]{2,1,0:T(8,128)S(1)}, u32[]{:S(2)}, u32[]{:S(2)}) collective-permute-start(f32[1,16,128]{2,1,0:T(8,128)S(1)} %get-tuple-element.36), channel_id=1, source_target_pairs={{0,8},{8,16},{16,24},{1,9},{9,17},{17,25},{2,10},{10,18},{18,26},{... | collective-permute-start | bytes 24584 | tf_op jit(solution)/shard_map/ppermute | solution.py:21
  215.7 7.3 %collective-permute-start.19 = (f32[10,1,128]{2,1,0:T(1,128)S(1)}, f32[10,1,128]{2,1,0:T(1,128)S(1)}, u32[]{:S(2)}, u32[]{:S(2)}) collective-permute-start(f32[10,1,128]{2,1,0:T(1,128)S(1)} %get-tuple-element.25), channel_id=1, source_target_pairs={{0,1},{1,2},{2,3},{3,4},{4,5},{5,6},{6,7},{8,9},{9,10},{10,11},{11... | collective-permute-start | bytes 15368 | tf_op jit(solution)/shard_map/ppermute | solution.py:21
  218.0 5.1 %collective-permute-start.18 = (f32[10,1,128]{2,1,0:T(1,128)S(1)}, f32[10,1,128]{2,1,0:T(1,128)S(1)}, u32[]{:S(2)}, u32[]{:S(2)}) collective-permute-start(f32[10,1,128]{2,1,0:T(1,128)S(1)} %get-tuple-element.24), channel_id=1, source_target_pairs={{1,0},{2,1},{3,2},{4,3},{5,4},{6,5},{7,6},{9,8},{10,9},{11,10},{12... | collective-permute-start | bytes 15368 | tf_op jit(solution)/shard_map/ppermute | solution.py:23
  223.3 5.9 %collective-permute-start.20 = (f32[1,16,128]{2,1,0:T(8,128)S(1)}, f32[1,16,128]{2,1,0:T(8,128)S(1)}, u32[]{:S(2)}, u32[]{:S(2)}) collective-permute-start(f32[1,16,128]{2,1,0:T(8,128)S(1)} %get-tuple-element.35), channel_id=1, source_target_pairs={{8,0},{16,8},{24,16},{9,1},{17,9},{25,17},{10,2},{18,10},{26,18},{... | collective-permute-start | bytes 24584 | tf_op jit(solution)/shard_map/ppermute | solution.py:23
  224.6 5.9 %collective-permute-start.21 = (f32[1,16,128]{2,1,0:T(8,128)S(1)}, f32[1,16,128]{2,1,0:T(8,128)S(1)}, u32[]{:S(2)}, u32[]{:S(2)}) collective-permute-start(f32[1,16,128]{2,1,0:T(8,128)S(1)} %get-tuple-element.34), channel_id=1, source_target_pairs={{0,8},{8,16},{16,24},{1,9},{9,17},{17,25},{2,10},{10,18},{18,26},{... | collective-permute-start | bytes 24584 | tf_op jit(solution)/shard_map/ppermute | solution.py:21
  230.5 4.4 %collective-permute-start.23 = (f32[10,1,128]{2,1,0:T(1,128)S(1)}, f32[10,1,128]{2,1,0:T(1,128)S(1)}, u32[]{:S(2)}, u32[]{:S(2)}) collective-permute-start(f32[10,1,128]{2,1,0:T(1,128)S(1)} %get-tuple-element.23), channel_id=1, source_target_pairs={{0,1},{1,2},{2,3},{3,4},{4,5},{5,6},{6,7},{8,9},{9,10},{10,11},{11... | collective-permute-start | bytes 15368 | tf_op jit(solution)/shard_map/ppermute | solution.py:21
  233.6 5.4 %collective-permute-start.22 = (f32[10,1,128]{2,1,0:T(1,128)S(1)}, f32[10,1,128]{2,1,0:T(1,128)S(1)}, u32[]{:S(2)}, u32[]{:S(2)}) collective-permute-start(f32[10,1,128]{2,1,0:T(1,128)S(1)} %get-tuple-element.22), channel_id=1, source_target_pairs={{1,0},{2,1},{3,2},{4,3},{5,4},{6,5},{7,6},{9,8},{10,9},{11,10},{12... | collective-permute-start | bytes 15368 | tf_op jit(solution)/shard_map/ppermute | solution.py:23
  (6 other events, 123.2 us)
